TPU v7x, 128 devices: a whole 4x4x4 slice. The times are simulated.
128 devices in a mesh: row: 32 (over z, x, core), col: 4 (over y).
Axes of the slice: x: 4, y: 4, z: 4, core: 2. Of those that a mesh axis runs over, the one named last changes fastest.
Arguments:
- panel: float32 [256, 65536], P('col', 'row'), may hold values from -6 to 6
- cauchy: float32 [256, 256], replicated, may hold values from -1 to 1
- refl_v: float32 [2, 512, 256, 128], P(None, 'row'), may hold values from -1 to 1
- block_start: int32 [2], replicated, may hold values from 0 to 127
Outputs:
- eigvec_out: float32 [256, 65536], P('col', 'row')
All inputs are finite; a program needn't handle non-finite values.
Results may differ from a plain program's by a relative error of at most 0.0003.
Values sent between devices are 32-bit elements; how exact they have to be, the bound alone decides.
A program may use at most 128 MiB of HBM per device.

v0:
```python
import functools
import jax
import jax.numpy as jnp
from jax import lax
from jax.experimental import pallas as pl
from jax.experimental.pallas import tpu as pltpu
from jax.sharding import PartitionSpec as P

F32 = jnp.float32
BF = jnp.bfloat16
S = 128
MESH = pl.DeviceIdType.MESH
VMEM = pl.BlockSpec(memory_space=pltpu.VMEM)
SMEM = pl.BlockSpec(memory_space=pltpu.SMEM)
ANY = pl.BlockSpec(memory_space=pl.ANY)


def split(x):
    high = x.astype(BF)
    return high, (x - high.astype(F32)).astype(BF)


def dot(a, b):
    return jnp.dot(a, b, preferred_element_type=F32)


def wide(x):
    return jnp.concatenate(split(x), axis=1)


def square(x):
    row = wide(x)
    return jnp.concatenate([row, row], axis=0)


def fold(x):
    return x[:, :S] + x[:, S:]


def mul(a, b_high, b_low):
    high, low = split(a)
    return dot(high, b_high) + (dot(low, b_high) + dot(high, b_low))


def lanes(rows, size):
    lane = lax.broadcasted_iota(jnp.int32, (rows, S), 1) // size
    return [(lane == b).astype(F32) for b in range(S // size)]


def spread(x, masks, at):
    high, low = split(x)
    zero = jnp.zeros(high.shape, BF)
    rows = []
    for b in range(len(masks)):
        if at[b] is None:
            rows.append(jnp.concatenate([zero, zero], axis=1))
        else:
            mask = masks[at[b]]
            rows.append(jnp.concatenate([high * mask, low * mask], axis=1))
    top = jnp.concatenate(rows, axis=0)
    return jnp.concatenate([top, top], axis=0)


def unit_inverses(nils):
    f4, f2 = lanes(32, 32), lanes(64, 64)
    b4, b2 = [m.astype(BF) for m in f4], [m.astype(BF) for m in f2]
    row = lax.broadcasted_iota(jnp.int32, (32, S), 0)
    lane = lax.broadcasted_iota(jnp.int32, (32, S), 1)
    eye = (row == lax.rem(lane, 32)).astype(F32)
    diag4, diag2 = [0, 1, 2, 3], [0, 1]

    def pick(n, size, masks, at):
        part = None
        for b, mask in zip(at, masks):
            piece = n[b * size : (b + 1) * size] * mask
            part = piece if part is None else part + piece
        return part

    small = [pick(n, 32, f4, diag4) for n in nils]
    result = [eye - c for c in small]
    power = [fold(dot(wide(c), spread(c, b4, diag4))) for c in small]
    for _ in range(3):
        both = [
            fold(dot(wide(jnp.concatenate([p, r], axis=0)), spread(p, b4, diag4)))
            for p, r in zip(power, result)
        ]
        result = [r + b[32:] for r, b in zip(result, both)]
        power = [b[:32] for b in both]
    result = [r + fold(dot(wide(r), spread(p, b4, diag4))) for p, r in zip(power, result)]

    under = [pick(n, 32, [f4[0], f4[2]], [1, 3]) for n in nils]
    inner = [fold(dot(wide(u), spread(r, b4, diag4))) for u, r in zip(under, result)]
    outer = [
        fold(dot(wide(r), spread(t, b4, [None, 0, None, 2]))) for r, t in zip(result, inner)
    ]
    result = [
        jnp.concatenate([r * (f4[0] + f4[2]), r * (f4[1] + f4[3]) - o], axis=0)
        for r, o in zip(result, outer)
    ]
    under = [n[64:] * f2[0] for n in nils]
    inner = [fold(dot(wide(u), spread(r, b2, diag2))) for u, r in zip(under, result)]
    outer = [fold(dot(wide(r), spread(t, b2, [None, 0]))) for r, t in zip(result, inner)]
    return [
        jnp.concatenate([r * f2[0], r * f2[1] - o], axis=0) for r, o in zip(result, outer)
    ]


def reflectors(blocks):
    row = lax.broadcasted_iota(jnp.int32, (S, S), 0)
    col = lax.broadcasted_iota(jnp.int32, (S, S), 1)
    eye = (row == col).astype(F32)
    turned = [split(v.T) for v in blocks]
    quads = [dot(t[0], wide(v)) for t, v in zip(turned, blocks)]
    grams = [fold(q) + q[:, S:].T for q in quads]
    scale = [2.0 / jnp.sum(g * eye, axis=0, keepdims=True) for g in grams]
    nils = [jnp.where(row > col, g * s, 0.0) for g, s in zip(grams, scale)]
    result = unit_inverses(nils)
    scaled = [
        wide(fold(dot(wide(v * s), square(r)))) for v, s, r in zip(blocks, scale, result)
    ]
    return [
        dot(w, jnp.concatenate([t[0], t[0]], axis=0))
        + dot(w, jnp.concatenate([t[1], t[1]], axis=0))
        for w, t in zip(scaled, turned)
    ]


def window(left, right, by):
    lane = lax.broadcasted_iota(jnp.int32, left.shape, 1)
    turn = lax.rem(S - by, S)
    return jnp.where(
        lane < S - by, pltpu.roll(left, turn, 1), pltpu.roll(right, turn, 1)
    )


def kernel(
    inner, offset_ref, panel_ref, cauchy_ref, v_ref, out_ref,
    v_all, k_high, k_low, panels, turned, home, mid_map, mid_data, z_high, z_low, aligned,
    map_one, map_two, data_one, data_two,
    pair_m, chip_m, chips_m, layer_m, layers_m, own_b, pair_b, chip_b, chips_b, layer_b, layers_b,
    own_m, load_sem, ring_send, ring_sem, halo_send, halo_sem, scan_send, scan_sem,
):
    me, slabs = lax.axis_index("row"), lax.axis_size("row")
    col, cols = lax.axis_index("col"), lax.axis_size("col")
    steps = v_ref.shape[1]
    rows = panel_ref.shape[0]
    half = rows // 2
    group = 2 * inner
    outer = slabs // group
    core = lax.rem(me, 2)
    chip = lax.rem(me // 2, inner)
    layer = me // group
    right, left = lax.rem(col + 1, cols), lax.rem(col + cols - 1, cols)
    after, before = lax.rem(me + 1, slabs), lax.rem(me + slabs - 1, slabs)
    partner = me + 1 - 2 * core
    near = [layer * group + lax.rem(chip + s, inner) * 2 + core for s in range(1, inner)]
    apart = [lax.rem(me + s * group, slabs) for s in range(1, outer)]

    loads = []
    for i in range(4):
        sweep, at = i // 2, (i % 2) * (steps // 2)
        loads.append(
            pltpu.make_async_copy(
                v_ref.at[sweep, pl.ds(at, steps // 2)],
                v_all.at[pl.ds(1 + sweep * (steps + 3) + at, steps // 2)],
                load_sem.at[i],
            )
        )
    loads.append(pltpu.make_async_copy(panel_ref, panels.at[col], load_sem.at[4]))
    for copy in loads:
        copy.start()

    barrier = pltpu.get_barrier_semaphore()
    for peer in (right, left):
        pl.semaphore_signal(barrier, inc=1, device_id={"col": peer}, device_id_type=MESH)
    for peer in [after, before, partner] + near + apart:
        pl.semaphore_signal(barrier, inc=1, device_id={"row": peer}, device_id_type=MESH)
    pl.semaphore_wait(barrier, 5 + len(near) + len(apart))

    def send(source, target, send_sem, recv_sem, device):
        return pltpu.make_async_remote_copy(
            src_ref=source, dst_ref=target, send_sem=send_sem, recv_sem=recv_sem,
            device_id=device, device_id_type=MESH,
        )

    halos = [
        send(v_ref.at[0, steps - 1], v_all.at[0], halo_send.at[0], halo_sem.at[0], {"row": after}),
        send(v_ref.at[1, steps - 1], v_all.at[steps + 3], halo_send.at[1], halo_sem.at[1], {"row": after}),
        send(v_ref.at[0, pl.ds(0, 2)], v_all.at[pl.ds(steps + 1, 2)], halo_send.at[2], halo_sem.at[2], {"row": before}),
    ]
    for copy in halos:
        copy.start()

    top, low_half = pl.ds(0, half), pl.ds(half, half)

    def ring(i, slot, part, peer, source=None):
        return send(
            panels.at[slot, part] if source is None else source,
            panels.at[slot, part], ring_send.at[i], ring_sem.at[i], {"col": peer},
        )

    first_ring = [
        ring(0, col, top, right, panel_ref.at[top]),
        ring(1, col, low_half, left, panel_ref.at[low_half]),
        ring(2, col, low_half, right, panel_ref.at[low_half]),
        ring(3, col, top, left, panel_ref.at[top]),
    ]
    for copy in first_ring:
        copy.start()
    second_ring = [ring(4, left, top, right), ring(5, right, low_half, left)]

    last = slabs * steps - 3
    row = lax.broadcasted_iota(jnp.int32, (2 * S, 2 * S), 0)
    colm = lax.broadcasted_iota(jnp.int32, (2 * S, 2 * S), 1)
    eye2 = (row == colm).astype(F32)

    def form(spots, slots):
        moved = reflectors([v_all[at] for at in spots])
        for at, slot, x in zip(spots, slots, moved):
            active = (slot >= 0) & (slot <= last)
            high, low = split(eye2 - jnp.where(active, x, 0.0))
            k_high[at] = high
            k_low[at] = low

    for copy in loads[:4]:
        copy.wait()

    def tick(t, _):
        at = 1 + 8 * t + 3 * (t // (steps // 8))
        k = lax.rem(t, steps // 8) * 8
        form([at + i for i in range(8)], [me * steps + k + i for i in range(8)])

        @pl.when(t == 2)
        def _():
            first_ring[0].wait_recv()
            second_ring[0].start()
            first_ring[1].wait_recv()
            second_ring[1].start()

        return 0

    lax.fori_loop(0, steps // 4, tick, 0)
    for copy in halos:
        copy.wait()
    form(
        [0, steps + 1, steps + 2, steps + 3],
        [me * steps - 1, me * steps + steps, me * steps + steps + 1, me * steps - 1],
    )

    o_one, o_two = offset_ref[0], offset_ref[1]
    reach = S + o_two - o_one
    jump = reach // S
    by = lax.rem(reach, S)
    eye = eye2[:S, :S]
    zero = jnp.zeros((S, S), F32)
    map_one[...] = eye
    map_two[...] = jnp.concatenate([zero, eye], axis=0)
    mid_map[0] = zero

    def map_step_one(k):
        high, low = k_high[k + 1, :S], k_low[k + 1, :S]
        out = mul(map_one[...], high, low)
        mid_map[k + 2] = out[:, :S]
        map_one[...] = out[:, S:]

    def map_step_two(k):
        fresh = window(mid_map[k + 2 + jump], mid_map[k + 3 + jump], by)
        x = jnp.concatenate([map_two[...], jnp.concatenate([fresh, zero], axis=0)], axis=1)
        out = mul(x, k_high[k + steps + 4], k_low[k + steps + 4])
        high, low = split(out[:, :S])
        z_high[k + 1] = high
        z_low[k + 1] = low
        map_two[...] = out[:, S:]

    def waves(one, two, save_one, save_two):
        for k in range(-1, 2):
            one(k)

        def both(k, _):
            one(k)
            two(k - 3)
            return 0

        lax.fori_loop(2, steps - 1, both, 0)
        save_one()
        lax.fori_loop(steps - 1, steps + 2, both, 0)
        save_two()
        two(steps - 1)

    def save_map_one():
        own_m[0] = map_one[...]

    def save_map_two():
        own_m[1] = map_two[:S]
        own_m[2] = map_two[S:]

    waves(map_step_one, map_step_two, save_map_one, save_map_two)

    def matrix(ref):
        high0, low0 = split(jnp.concatenate([ref[0], ref[1]], axis=1))
        high1, low1 = split(jnp.concatenate([zero, ref[2]], axis=1))
        return jnp.concatenate([high0, high1], axis=0), jnp.concatenate([low0, low1], axis=0)

    def whole(ref):
        return jnp.concatenate(
            [jnp.concatenate([ref[0], ref[1]], axis=1), jnp.concatenate([zero, ref[2]], axis=1)], axis=0
        )

    def keep(ref, x):
        ref[0] = x[:S, :S]
        ref[1] = x[:S, S:]
        ref[2] = x[S:, S:]

    pair = send(own_m, pair_m, scan_send.at[0], scan_sem.at[0], {"row": partner})
    pair.start()

    turned[...] = cauchy_ref[...].T
    loads[4].wait()
    for copy in first_ring[2:]:
        copy.wait_recv()
    for copy in second_ring:
        copy.wait_recv()
    mix_high, mix_low = split(turned[pl.ds(pl.multiple_of(col * rows, rows), rows)])
    mix = jnp.concatenate([mix_high, mix_low], axis=0)
    home[0] = jnp.zeros((rows, S), F32)

    def merge(j, _):
        at = pl.ds(pl.multiple_of(j * S, S), S)
        part = jnp.concatenate([panels[c, :, at] for c in range(cols)], axis=0)
        both = dot(mix, wide(part))
        home[j + 1] = fold(both[:rows]) + fold(both[rows:])
        return 0

    lax.fori_loop(0, 4, merge, 0)
    margin = send(
        home.at[pl.ds(1, 4)], home.at[pl.ds(steps + 1, 4)], halo_send.at[3], halo_sem.at[3], {"row": before}
    )
    margin.start()
    lax.fori_loop(4, steps, merge, 0)

    pair.wait()
    on_first = core == 0
    first_m = jnp.where(on_first, whole(own_m), whole(pair_m))
    second_m = jnp.where(on_first, whole(pair_m), whole(own_m))
    keep(chip_m, mul(first_m, *split(second_m)))
    chip_sends = []
    for s in range(1, inner):
        chip_sends.append(
            send(chip_m, chips_m.at[chip], scan_send.at[s], scan_sem.at[s], {"row": near[s - 1]})
        )
        chip_sends[-1].start()
    chips_m[chip] = chip_m[...]
    margin.wait()

    def fresh_one(k):
        return window(home[k + 1], home[k + 2], o_one)

    is_first = me == 0
    data_one[...] = jnp.where(is_first, fresh_one(-1), 0.0)
    mid_data[0] = jnp.zeros((rows, S), F32)

    def data_step_one(k):
        x = jnp.concatenate([data_one[...], fresh_one(k + 1)], axis=1)
        out = mul(x, k_high[k + 1], k_low[k + 1])
        mid_data[k + 2] = out[:, :S]
        data_one[...] = out[:, S:]

    def fresh_two(k):
        return window(mid_data[k + 1 + jump], mid_data[k + 2 + jump], by)

    def data_step_two(k):
        carried = data_two[...]
        if not isinstance(k, int):
            carried = jnp.where(is_first & (k == -1), fresh_two(-1), carried)
        x = jnp.concatenate([carried, fresh_two(k + 1)], axis=1)
        out = mul(x, k_high[k + steps + 4], k_low[k + steps + 4])
        aligned[k + 1] = out[:, :S]
        data_two[...] = out[:, S:]

    data_two[...] = jnp.zeros((rows, S), F32)

    def save_data_one():
        own_b[:, :S] = data_one[...]

    def save_data_two():
        own_b[:, S:] = data_two[...]

    waves(data_step_one, data_step_two, save_data_one, save_data_two)

    pair = send(own_b, pair_b, scan_send.at[inner], scan_sem.at[inner], {"row": partner})
    pair.start()

    for copy in chip_sends:
        copy.wait()
    total = whole(chips_m.at[0])
    lead = eye2
    for j in range(1, inner):
        lead = jnp.where(chip == j, total, lead)
        total = mul(total, *matrix(chips_m.at[j]))
    keep(layer_m, total)
    at = inner + 1
    layer_sends = []
    for s in range(1, outer):
        layer_sends.append(
            send(layer_m, layers_m.at[layer], scan_send.at[at], scan_sem.at[at], {"row": apart[s - 1]})
        )
        layer_sends[-1].start()
        at += 1
    layers_m[layer] = layer_m[...]

    pair.wait()
    first_b = jnp.where(on_first, own_b[...], pair_b[...])
    second_b = jnp.where(on_first, pair_b[...], own_b[...])
    chip_b[...] = mul(first_b, *split(second_m)) + second_b
    chip_sends = []
    for s in range(1, inner):
        chip_sends.append(
            send(chip_b, chips_b.at[chip], scan_send.at[at], scan_sem.at[at], {"row": near[s - 1]})
        )
        chip_sends[-1].start()
        at += 1
    chips_b[chip] = chip_b[...]
    lead_m = jnp.where(on_first, lead, mul(lead, *split(first_m)))
    for copy in chip_sends:
        copy.wait()
    total_b = chips_b[0]
    lead_b = jnp.zeros((rows, 2 * S), F32)
    for j in range(1, inner):
        lead_b = jnp.where(chip == j, total_b, lead_b)
        total_b = mul(total_b, *matrix(chips_m.at[j])) + chips_b[j]
    layer_b[...] = total_b
    last_sends = []
    for s in range(1, outer):
        last_sends.append(
            send(layer_b, layers_b.at[layer], scan_send.at[at], scan_sem.at[at], {"row": apart[s - 1]})
        )
        last_sends[-1].start()
        at += 1
    layers_b[layer] = layer_b[...]
    lead_b = jnp.where(on_first, lead_b, mul(lead_b, *split(first_m)) + first_b)
    for copy in layer_sends:
        copy.wait()
    for copy in last_sends:
        copy.wait()
    carry = jnp.zeros((rows, 2 * S), F32)
    for z in range(outer - 1):
        longer = mul(carry, *matrix(layers_m.at[z])) + layers_b[z]
        carry = jnp.where(z < layer, longer, carry)
    carry = mul(carry, *split(lead_m)) + lead_b

    high, low = split(carry)
    both = jnp.concatenate([high, low], axis=0)
    for j in range(steps + 1):
        part = dot(both, z_high[j])
        aligned[j] = aligned[j] + (part[:rows] + (part[rows:] + dot(high, z_low[j])))
    reach_out = S - o_two
    jump_out = reach_out // S
    by_out = lax.rem(reach_out, S)
    for j in range(steps):
        out_ref[:, j * S : (j + 1) * S] = window(
            aligned[j + jump_out], aligned[j + jump_out + 1], by_out
        )
    for copy in first_ring + second_ring:
        copy.wait_send()


def shards(panel, cauchy, refl_v, block_start):
    rows, width = panel.shape
    steps = refl_v.shape[1]
    cols, slabs = lax.axis_size("col"), lax.axis_size("row")
    inner = 4
    outer = slabs // (2 * inner)
    count = 2 * steps + 4
    scan_copies = 2 + 2 * (inner - 1) + 2 * (outer - 1)

    def f(*shape):
        return pltpu.VMEM(shape, F32)

    def b(*shape):
        return pltpu.VMEM(shape, BF)

    dma = pltpu.SemaphoreType.DMA
    return pl.pallas_call(
        functools.partial(kernel, inner),
        in_specs=[SMEM, ANY, VMEM, ANY],
        out_specs=VMEM,
        out_shape=jax.ShapeDtypeStruct((rows, width), F32),
        scratch_shapes=[
            f(count, 2 * S, S), b(count, 2 * S, 2 * S), b(count, 2 * S, 2 * S),
            f(cols, rows, width), f(2 * S, 2 * S), f(steps + 5, rows, S),
            f(steps + 5, S, S), f(steps + 5, rows, S),
            b(steps + 1, 2 * S, S), b(steps + 1, 2 * S, S), f(steps + 2, rows, S),
            f(S, S), f(2 * S, S), f(rows, S), f(rows, S),
            f(3, S, S), f(3, S, S), f(inner, 3, S, S), f(3, S, S), f(outer, 3, S, S),
            f(rows, 2 * S), f(rows, 2 * S), f(rows, 2 * S), f(inner, rows, 2 * S),
            f(rows, 2 * S), f(outer, rows, 2 * S), f(3, S, S),
            dma((5,)), dma((6,)), dma((6,)), dma((4,)), dma((4,)),
            dma((scan_copies,)), dma((scan_copies,)),
        ],
        compiler_params=pltpu.CompilerParams(
            collective_id=0, has_side_effects=True, vmem_limit_bytes=60 * 2**20
        ),
        name="back_transform",
    )(block_start, panel, cauchy, refl_v)


def solution(mesh):
    placed = (P("col", "row"), P(), P(None, "row", None, None), P())
    return jax.shard_map(
        shards, mesh=mesh, in_specs=placed, out_specs=P("col", "row"), check_vma=False
    )
```

profile of v0, /device:TPU:1, one launch (start us, length us, event | category | flops | bytes accessed | tf_op | source)
XLA Modules:
  0.0 68.4 jit_solution(6889597555740388320)
XLA Ops:
  0.0 66.6 %back_transform.1 = f32[64,2048]{1,0:T(8,128)} custom-call(s32[2]{0:T(128)} %offset_ref.1, f32[64,2048]{1,0:T(8,128)} %panel_ref.1, f32[256,256]{1,0:T(8,128)} %cauchy_ref.1, f32[2,16,256,128]{3,2,1,0:T(8,128)} %v_ref.1), custom_call_target="tpu_custom_call" | custom-call | tf_op jit(solution)/shard_map/back_transform/pallas_call | solution.py:483
  66.6 1.9 %copy.6 = f32[64,2048]{1,0:T(8,128)} copy(f32[64,2048]{1,0:T(8,128)} %back_transform.1) | data formatting | bytes 1048576
where the time goes:
time: 69 us; the launch traced here: 68.4 us
  Pallas kernels  66.6 us (97%)
  local copies, waits for them, and re-layouts  1.87 us (3%)
    pallas_call x1, Pallas kernels, shards(): pl.pallas_call(functools.partial(kernel, inner), in_specs=[SMEM, ANY, VME...  66.6 us
    unnamed x1, local copies, waits for them, and re-layouts  1.87 us

commit v1 on v0

v1 whole, which is shorter than its diff:
```python
import functools
import jax
import jax.numpy as jnp
from jax import lax
from jax.experimental import pallas as pl
from jax.experimental.pallas import tpu as pltpu
from jax.sharding import PartitionSpec as P

F32 = jnp.float32
BF = jnp.bfloat16
S = 128
MESH = pl.DeviceIdType.MESH
VMEM = pl.BlockSpec(memory_space=pltpu.VMEM)
SMEM = pl.BlockSpec(memory_space=pltpu.SMEM)
ANY = pl.BlockSpec(memory_space=pl.ANY)


def split(x):
    high = x.astype(BF)
    return high, (x - high.astype(F32)).astype(BF)


def dot(a, b):
    return jnp.dot(a, b, preferred_element_type=F32)


def dot_t(a, b):
    return lax.dot_general(a, b, (((1,), (1,)), ((), ())), preferred_element_type=F32)


def wide(x):
    return jnp.concatenate(split(x), axis=1)


def square(x):
    row = wide(x)
    return jnp.concatenate([row, row], axis=0)


def fold(x):
    return x[:, :S] + x[:, S:]


def mul(a, b_high, b_low):
    high, low = split(a)
    return dot(
        jnp.concatenate([high, low, high], axis=1), jnp.concatenate([b_high, b_high, b_low], axis=0)
    )


def lanes(rows, size):
    lane = lax.broadcasted_iota(jnp.int32, (rows, S), 1) // size
    return [(lane == b).astype(F32) for b in range(S // size)]


def spread(x, masks, at):
    high, low = split(x)
    zero = jnp.zeros(high.shape, BF)
    rows = []
    for b in range(len(masks)):
        if at[b] is None:
            rows.append(jnp.concatenate([zero, zero], axis=1))
        else:
            mask = masks[at[b]]
            rows.append(jnp.concatenate([high * mask, low * mask], axis=1))
    top = jnp.concatenate(rows, axis=0)
    return jnp.concatenate([top, top], axis=0)


def unit_inverses(nils):
    f4, f2 = lanes(32, 32), lanes(64, 64)
    b4, b2 = [m.astype(BF) for m in f4], [m.astype(BF) for m in f2]
    row = lax.broadcasted_iota(jnp.int32, (32, S), 0)
    lane = lax.broadcasted_iota(jnp.int32, (32, S), 1)
    eye = (row == lax.rem(lane, 32)).astype(F32)
    diag4, diag2 = [0, 1, 2, 3], [0, 1]

    def pick(n, size, masks, at):
        part = None
        for b, mask in zip(at, masks):
            piece = n[b * size : (b + 1) * size] * mask
            part = piece if part is None else part + piece
        return part

    small = [pick(n, 32, f4, diag4) for n in nils]
    result = [eye - c for c in small]
    power = [fold(dot(wide(c), spread(c, b4, diag4))) for c in small]
    yield
    for _ in range(3):
        both = [
            fold(dot(wide(jnp.concatenate([p, r], axis=0)), spread(p, b4, diag4)))
            for p, r in zip(power, result)
        ]
        result = [r + b[32:] for r, b in zip(result, both)]
        power = [b[:32] for b in both]
        yield
    result = [r + fold(dot(wide(r), spread(p, b4, diag4))) for p, r in zip(power, result)]
    yield

    under = [pick(n, 32, [f4[0], f4[2]], [1, 3]) for n in nils]
    inner = [fold(dot(wide(u), spread(r, b4, diag4))) for u, r in zip(under, result)]
    yield
    outer = [
        fold(dot(wide(r), spread(t, b4, [None, 0, None, 2]))) for r, t in zip(result, inner)
    ]
    result = [
        jnp.concatenate([r * (f4[0] + f4[2]), r * (f4[1] + f4[3]) - o], axis=0)
        for r, o in zip(result, outer)
    ]
    yield
    under = [n[64:] * f2[0] for n in nils]
    inner = [fold(dot(wide(u), spread(r, b2, diag2))) for u, r in zip(under, result)]
    yield
    outer = [fold(dot(wide(r), spread(t, b2, [None, 0]))) for r, t in zip(result, inner)]
    return [
        jnp.concatenate([r * f2[0], r * f2[1] - o], axis=0) for r, o in zip(result, outer)
    ]


def prepare(blocks, active):
    row = lax.broadcasted_iota(jnp.int32, (S, S), 0)
    col = lax.broadcasted_iota(jnp.int32, (S, S), 1)
    eye = (row == col).astype(F32)
    quads = [dot(v.T.astype(BF), wide(v)) for v in blocks]
    yield
    grams = [fold(q) + q[:, S:].T for q in quads]
    scale = [
        jnp.where(on, -2.0 / jnp.sum(g * eye, axis=0, keepdims=True), 0.0)
        for g, on in zip(grams, active)
    ]
    nils = [jnp.where(row > col, g * -s, 0.0) for g, s in zip(grams, scale)]
    yield
    result = yield from unit_inverses(nils)
    return scale, result


def less(v, scale, result):
    high, low = split(fold(dot(wide(v * scale), square(result))))
    v_high, v_low = split(v)
    both = jnp.concatenate([high, low], axis=1)
    return dot_t(both, jnp.concatenate([v_high, v_high], axis=1)) + dot_t(high, v_low)


def window(left, right, by):
    lane = lax.broadcasted_iota(jnp.int32, left.shape, 1)
    turn = lax.rem(S - by, S)
    return jnp.where(
        lane < S - by, pltpu.roll(left, turn, 1), pltpu.roll(right, turn, 1)
    )


def kernel(
    inner, offset_ref, panel_ref, cauchy_ref, v_ref, out_ref,
    v_all, k_high, k_low, panels, turned, home, mid_map, mid_data, z_high, z_low, aligned,
    map_one, map_two, data_one, data_two,
    pair_m, chip_m, chips_m, layer_m, layers_m, own_b, pair_b, chip_b, chips_b, layer_b, layers_b,
    own_m, ready_s, ready_r, load_sem, ring_send, ring_sem, halo_send, halo_sem, scan_send, scan_sem,
):
    me, slabs = lax.axis_index("row"), lax.axis_size("row")
    col, cols = lax.axis_index("col"), lax.axis_size("col")
    steps = v_ref.shape[1]
    rows = panel_ref.shape[0]
    half = rows // 2
    group = 2 * inner
    outer = slabs // group
    core = lax.rem(me, 2)
    chip = lax.rem(me // 2, inner)
    layer = me // group
    right, left = lax.rem(col + 1, cols), lax.rem(col + cols - 1, cols)
    after, before = lax.rem(me + 1, slabs), lax.rem(me + slabs - 1, slabs)
    partner = me + 1 - 2 * core
    near = [layer * group + lax.rem(chip + s, inner) * 2 + core for s in range(1, inner)]
    apart = [lax.rem(me + s * group, slabs) for s in range(1, outer)]

    loads = []
    for i in range(4):
        sweep, at = i // 2, (i % 2) * (steps // 2)
        loads.append(
            pltpu.make_async_copy(
                v_ref.at[sweep, pl.ds(at, steps // 2)],
                v_all.at[pl.ds(1 + sweep * (steps + 3) + at, steps // 2)],
                load_sem.at[i],
            )
        )
    loads.append(pltpu.make_async_copy(panel_ref, panels.at[col], load_sem.at[4]))
    loads[0].start()

    barrier = pltpu.get_barrier_semaphore()
    for peer in (right, left):
        pl.semaphore_signal(barrier, inc=1, device_id={"col": peer}, device_id_type=MESH)
    for peer in [after, before, partner] + near + apart:
        pl.semaphore_signal(barrier, inc=1, device_id={"row": peer}, device_id_type=MESH)

    def send(source, target, send_sem, recv_sem, device):
        return pltpu.make_async_remote_copy(
            src_ref=source, dst_ref=target, send_sem=send_sem, recv_sem=recv_sem,
            device_id=device, device_id_type=MESH,
        )

    halos = [
        send(v_ref.at[0, steps - 1], v_all.at[0], halo_send.at[0], halo_sem.at[0], {"row": after}),
        send(v_ref.at[1, steps - 1], v_all.at[steps + 3], halo_send.at[1], halo_sem.at[1], {"row": after}),
        send(v_ref.at[0, pl.ds(0, 2)], v_all.at[pl.ds(steps + 1, 2)], halo_send.at[2], halo_sem.at[2], {"row": before}),
    ]

    class Ring:
        def __init__(self, source, slots, place, size, axis, peer, parts, send_sem, recv_sem, base):
            ahead, behind = lax.rem(place + 1, size), lax.rem(place + size - 1, size)
            up, down = {axis: peer(ahead)}, {axis: peer(behind)}
            one, two = parts
            sems = iter(range(base, base + 6))

            def copy(slot, part, device, own):
                i = next(sems)
                target = slots.at[(slot, *part)]
                return send(source.at[part] if own else target, target, send_sem.at[i], recv_sem.at[i], device)

            self.first = [
                copy(place, one, up, True), copy(place, two, down, True),
                copy(place, two, up, True), copy(place, one, down, True),
            ]
            self.second = [copy(behind, one, up, False), copy(ahead, two, down, False)]

        def start(self):
            for copy in self.first:
                copy.start()

        def forward(self):
            for arrived, onward in zip(self.first, self.second):
                arrived.wait_recv()
                onward.start()

        def arrive(self):
            for copy in self.first[2:] + self.second:
                copy.wait_recv()

        def finish(self):
            for copy in self.first + self.second:
                copy.wait_send()

    class SplitRing(Ring):
        def __init__(self, source, slots, place, size, axis, peer, send_sem, recv_sem, base):
            at, quarter = core * (S // 2), S // 4
            parts = [(slice(None), pl.ds(pl.multiple_of(at + i * quarter, quarter), quarter)) for i in range(2)]
            super().__init__(source, slots, place, size, axis, peer, parts, send_sem, recv_sem, base)
            rows_here = pl.ds(pl.multiple_of(at, S // 2), S // 2)
            self.swaps = []
            for i, shift in enumerate((size - 1, 1, 2)):
                ref = slots.at[lax.rem(place + shift, size), :, rows_here]
                self.swaps.append(
                    send(ref, ref, send_sem.at[base + 6 + i], recv_sem.at[base + 6 + i], {"row": partner})
                )

        def swap_near(self):
            for copy, swap in zip(self.first[2:], self.swaps):
                copy.wait_recv()
                swap.start()

        def swap_far(self):
            for copy in self.second:
                copy.wait_recv()
            self.swaps[2].start()

        def arrive(self):
            for swap in self.swaps:
                swap.wait_recv()

        def finish(self):
            for copy in self.first + self.second + self.swaps:
                copy.wait_send()

    class Direct:
        def __init__(self, source, slots, place, size, axis, peer, send_sem, recv_sem, base):
            mine = pl.ds(pl.multiple_of(core * half, half), half)
            to = [{axis: peer(lax.rem(place + shift, size))} for shift in (2, 1, size - 1)]
            refs = [(source.at[mine], slots.at[place, mine])] + [(source, slots.at[place])] * 2
            self.copies = [
                send(*ref, send_sem.at[base + i], recv_sem.at[base + i], device)
                for i, (ref, device) in enumerate(zip(refs, to))
            ]
            ref = slots.at[lax.rem(place + 2, size), mine]
            self.swap = send(ref, ref, send_sem.at[base + 3], recv_sem.at[base + 3], {"row": partner})

        def start(self):
            for copy in self.copies:
                copy.start()

        def relay(self):
            self.copies[0].wait_recv()
            self.swap.start()

        def arrive(self):
            for copy in [*self.copies[1:], self.swap]:
                copy.wait_recv()

        def finish(self):
            for copy in [*self.copies, self.swap]:
                copy.wait_send()

    flat = [(pl.ds(i * half, half),) for i in range(2)]
    width = panel_ref.shape[1] // 2
    panel_rings = []
    for i in range(2):
        parts = [(*rows_of, pl.ds(i * width, width)) for rows_of in flat]
        panel_rings.append(
            Ring(panel_ref, panels, col, cols, "col", lambda c: c, parts, ring_send, ring_sem, 6 * i)
        )
    in_layer = dict(place=chip, size=inner, axis="row", peer=lambda x: layer * group + 2 * x + core)
    over_layers = dict(place=layer, size=outer, axis="row", peer=lambda z: z * group + 2 * chip + core)

    scan_sems = dict(send_sem=scan_send, recv_sem=scan_sem)
    chip_ring_m = SplitRing(chip_m, chips_m, base=2, **in_layer, **scan_sems)
    layer_ring_m = SplitRing(layer_m, layers_m, base=11, **over_layers, **scan_sems)
    chip_ring_b = Direct(chip_b, chips_b, base=20, **in_layer, **scan_sems)
    layer_ring_b = Direct(layer_b, layers_b, base=24, **over_layers, **scan_sems)

    last = slabs * steps - 3
    row = lax.broadcasted_iota(jnp.int32, (2 * S, 2 * S), 0)
    colm = lax.broadcasted_iota(jnp.int32, (2 * S, 2 * S), 1)
    eye2 = (row == colm).astype(F32)

    def is_on(slot):
        return (slot >= 0) & (slot <= last)

    def begin(batch, filler):
        stages = prepare([v_all[at] for at, _ in batch], [is_on(slot) for _, slot in batch])
        share = -(-len(filler) // 9)
        filler = list(filler)
        while True:
            try:
                next(stages)
            except StopIteration as done:
                scale, result = done.value
                break
            for piece in filler[:share]:
                piece()
            filler = filler[share:]
        for piece in filler:
            piece()
        for i in range(len(batch)):
            ready_s[i] = jnp.broadcast_to(scale[i], (8, S))
            ready_r[i] = result[i]

    def end(i, at):
        x = less(v_all[at], ready_s[i, :1], ready_r[i])
        for r in range(2):
            for c in range(2):
                here = pl.ds(r * S, S), pl.ds(c * S, S)
                part = x[r * S : (r + 1) * S, c * S : (c + 1) * S]
                high, low = split(eye2[:S, :S] + part if r == c else part)
                k_high[(at, *here)] = high
                k_low[(at, *here)] = low

    def ends(batch):
        return [functools.partial(end, i, at) for i, (at, _) in enumerate(batch)]

    first_slot = me * steps

    def batch_of(t):
        at, slot = 1 + 8 * t + 3 * (t // (steps // 8)), first_slot + lax.rem(t, steps // 8) * 8
        return [(at + i, slot + i) for i in range(8)]

    seam = [(0, first_slot - 1), (steps + 3, first_slot - 1)]
    seam += [(steps + 1, first_slot + steps), (steps + 2, first_slot + steps + 1)]

    o_one, o_two = offset_ref[0], offset_ref[1]
    reach = S + o_two - o_one
    jump = reach // S
    by = lax.rem(reach, S)
    eye = eye2[:S, :S]
    zero = jnp.zeros((S, S), F32)
    map_one[...] = eye
    map_two[...] = jnp.concatenate([zero, eye], axis=0)
    mid_map[0] = zero

    def map_step_one(k):
        out = mul(map_one[...], k_high[k + 1, :S], k_low[k + 1, :S])
        mid_map[k + 2] = out[:, :S]
        map_one[...] = out[:, S:]

    def map_step_two(k):
        fresh = window(mid_map[k + 2 + jump], mid_map[k + 3 + jump], by)
        at = k + steps + 4
        x = jnp.concatenate([map_two[...], jnp.concatenate([fresh, zero], axis=0)], axis=1)
        out = mul(x, k_high[at], k_low[at])
        z_high[k + 1], z_low[k + 1] = split(out[:, :S])
        map_two[...] = out[:, S:]

    def wave(k, one, two, save_one, save_two):
        if k < steps + 2:
            one(k)
        if k > 1:
            two(k - 3)
        if k == steps - 2:
            save_one()
        if k == steps + 1:
            save_two()

    def save_map_one():
        own_m[0] = map_one[...]

    def save_map_two():
        own_m[1] = map_two[:S]
        own_m[2] = map_two[S:]

    def map_waves(ks):
        return [functools.partial(wave, k, map_step_one, map_step_two, save_map_one, save_map_two) for k in ks]

    def mixed(some, others):
        out = []
        while some or others:
            out += some[:1] + others[:1]
            some, others = some[1:], others[1:]
        return out

    def enter():
        pl.semaphore_wait(barrier, 5 + len(near) + len(apart))
        for copy in halos:
            copy.start()
        panel_rings[0].start()

    loads[0].wait()
    for copy in loads[1:]:
        copy.start()
    begin(batch_of(0), [])
    enter()
    for copy in loads[1:4]:
        copy.wait()

    def tick(t, _):
        @pl.when(t == 3)
        def _():
            panel_rings[0].forward()
            panel_rings[1].start()

        begin(batch_of(t), ends(batch_of(t - 1)))
        return 0

    lax.fori_loop(1, steps // 4, tick, 0)
    for copy in halos:
        copy.wait()
    begin(seam, ends(batch_of(steps // 4 - 1)))
    turned[...] = cauchy_ref[...].T
    mix_high, mix_low = split(turned[pl.ds(pl.multiple_of(col * rows, rows), rows)])
    mix = jnp.concatenate([mix_high, mix_low], axis=0)
    home[0] = jnp.zeros((rows, S), F32)

    def merge(j, _):
        at = pl.ds(pl.multiple_of(j * S, S), S)
        part = jnp.concatenate([panels[c, :, at] for c in range(cols)], axis=0)
        both = dot(mix, wide(part))
        home[j + 1] = fold(both[:rows]) + fold(both[rows:])
        return 0

    margin = send(
        home.at[pl.ds(1, 4)], home.at[pl.ds(steps + 1, 4)], halo_send.at[3], halo_sem.at[3], {"row": before}
    )

    def merge_first():
        loads[4].wait()
        panel_rings[0].arrive()
        lax.fori_loop(0, steps // 2, merge, 0, unroll=4)

        @pl.when(me > 0)
        def _():
            margin.start()

        @pl.when(me == slabs - 1)
        def _():
            home[pl.ds(steps + 1, 4)] = jnp.zeros((4, rows, S), F32)


    for piece in ends(seam):
        piece()
    merge_first()
    for piece in map_waves(range(-1, 9)):
        piece()
    panel_rings[1].forward()
    for piece in map_waves(range(9, steps + 3)):
        piece()

    def matrix(ref):
        high0, low0 = split(jnp.concatenate([ref[0], ref[1]], axis=1))
        high1, low1 = split(jnp.concatenate([zero, ref[2]], axis=1))
        return jnp.concatenate([high0, high1], axis=0), jnp.concatenate([low0, low1], axis=0)

    def whole(ref):
        return jnp.concatenate(
            [jnp.concatenate([ref[0], ref[1]], axis=1), jnp.concatenate([zero, ref[2]], axis=1)], axis=0
        )

    def keep(ref, x):
        ref[0] = x[:S, :S]
        ref[1] = x[:S, S:]
        ref[2] = x[S:, S:]

    pair = send(own_m, pair_m, scan_send.at[0], scan_sem.at[0], {"row": partner})
    pair.start()

    pair.wait()
    on_first = core == 0
    first_m = jnp.where(on_first, whole(own_m), whole(pair_m))
    second_m = jnp.where(on_first, whole(pair_m), whole(own_m))
    keep(chip_m, mul(first_m, *split(second_m)))
    chip_ring_m.start()
    chips_m[chip] = chip_m[...]

    def fresh_one(k):
        return window(home[k + 1], home[k + 2], o_one)

    is_first = me == 0
    data_one[...] = jnp.where(is_first, fresh_one(-1), 0.0)
    mid_data[0] = jnp.zeros((rows, S), F32)

    def data_step_one(k):
        x = jnp.concatenate([data_one[...], fresh_one(k + 1)], axis=1)
        out = mul(x, k_high[k + 1], k_low[k + 1])
        mid_data[k + 2] = out[:, :S]
        data_one[...] = out[:, S:]

    def fresh_two(k):
        return window(mid_data[k + 1 + jump], mid_data[k + 2 + jump], by)

    def data_step_two(k):
        carried = data_two[...] if k >= 0 else jnp.where(is_first, fresh_two(-1), 0.0)
        x = jnp.concatenate([carried, fresh_two(k + 1)], axis=1)
        out = mul(x, k_high[k + steps + 4], k_low[k + steps + 4])
        aligned[k + 1] = out[:, :S]
        data_two[...] = out[:, S:]


    def save_data_one():
        own_b[:, :S] = data_one[...]

    def save_data_two():
        own_b[:, S:] = data_two[...]

    def merge_second():
        panel_rings[1].arrive()
        lax.fori_loop(steps // 2, steps, merge, 0, unroll=4)

    def take_margin():
        @pl.when(me < slabs - 1)
        def _():
            margin.wait_recv()

    also = {
        4: merge_second, 7: chip_ring_m.forward, 11: chip_ring_m.swap_near, steps - 2: take_margin,
        steps + 1: chip_ring_m.swap_far,
    }
    for k in range(-1, steps + 3):
        if k in also:
            also[k]()
        wave(k, data_step_one, data_step_two, save_data_one, save_data_two)

    pair = send(own_b, pair_b, scan_send.at[1], scan_sem.at[1], {"row": partner})
    pair.start()

    chip_ring_m.arrive()
    total = whole(chips_m.at[0])
    lead = eye2
    for j in range(1, inner):
        lead = jnp.where(chip == j, total, lead)
        total = mul(total, *matrix(chips_m.at[j]))
    keep(layer_m, total)
    layer_ring_m.start()
    layers_m[layer] = layer_m[...]

    pair.wait()
    first_b = jnp.where(on_first, own_b[...], pair_b[...])
    second_b = jnp.where(on_first, pair_b[...], own_b[...])
    chip_b[...] = mul(first_b, *split(second_m)) + second_b
    chip_ring_b.start()
    chips_b[chip] = chip_b[...]
    lead_m = jnp.where(on_first, lead, mul(lead, *split(first_m)))
    chip_ring_b.relay()
    layer_ring_m.forward()
    layer_ring_m.swap_near()
    chip_ring_b.arrive()
    total_b = chips_b[0]
    lead_b = jnp.zeros((rows, 2 * S), F32)
    for j in range(1, inner):
        lead_b = jnp.where(chip == j, total_b, lead_b)
        total_b = mul(total_b, *matrix(chips_m.at[j])) + chips_b[j]
    layer_b[...] = total_b
    layer_ring_b.start()
    layers_b[layer] = layer_b[...]
    lead_b = jnp.where(on_first, lead_b, mul(lead_b, *split(first_m)) + first_b)
    layer_ring_m.swap_far()
    layer_ring_b.relay()
    layer_ring_m.arrive()
    layer_ring_b.arrive()
    carry = jnp.zeros((rows, 2 * S), F32)
    for z in range(outer - 1):
        longer = mul(carry, *matrix(layers_m.at[z])) + layers_b[z]
        carry = jnp.where(z < layer, longer, carry)
    carry = mul(carry, *split(lead_m)) + lead_b

    high, low = split(carry)
    both = jnp.concatenate([high, low], axis=0)
    for j in range(steps + 1):
        part = dot(both, z_high[j])
        aligned[j] = aligned[j] + (part[:rows] + (part[rows:] + dot(high, z_low[j])))
    reach_out = S - o_two
    jump_out = reach_out // S
    by_out = lax.rem(reach_out, S)
    for j in range(steps):
        out_ref[:, j * S : (j + 1) * S] = window(
            aligned[j + jump_out], aligned[j + jump_out + 1], by_out
        )
    for ring in (*panel_rings, chip_ring_m, chip_ring_b, layer_ring_m, layer_ring_b):
        ring.finish()

    @pl.when(me > 0)
    def _():
        margin.wait_send()


def shards(panel, cauchy, refl_v, block_start):
    rows, width = panel.shape
    steps = refl_v.shape[1]
    cols, slabs = lax.axis_size("col"), lax.axis_size("row")
    inner = 4
    outer = slabs // (2 * inner)
    count = 2 * steps + 4
    scan_copies = 2 + 2 * 9 + 2 * 4

    def f(*shape):
        return pltpu.VMEM(shape, F32)

    def b(*shape):
        return pltpu.VMEM(shape, BF)

    dma = pltpu.SemaphoreType.DMA
    return pl.pallas_call(
        functools.partial(kernel, inner),
        in_specs=[SMEM, ANY, VMEM, ANY],
        out_specs=VMEM,
        out_shape=jax.ShapeDtypeStruct((rows, width), F32),
        scratch_shapes=[
            f(count, 2 * S, S), b(count, 2 * S, 2 * S), b(count, 2 * S, 2 * S),
            f(cols, rows, width), f(2 * S, 2 * S), f(steps + 5, rows, S),
            f(steps + 5, S, S), f(steps + 5, rows, S),
            b(steps + 1, 2 * S, S), b(steps + 1, 2 * S, S), f(steps + 2, rows, S),
            f(S, S), f(2 * S, S), f(rows, S), f(rows, S),
            f(3, S, S), f(3, S, S), f(inner, 3, S, S), f(3, S, S), f(outer, 3, S, S),
            f(rows, 2 * S), f(rows, 2 * S), f(rows, 2 * S), f(inner, rows, 2 * S),
            f(rows, 2 * S), f(outer, rows, 2 * S), f(3, S, S),
            f(8, 8, S), f(8, S, S),
            dma((5,)), dma((12,)), dma((12,)), dma((4,)), dma((4,)),
            dma((scan_copies,)), dma((scan_copies,)),
        ],
        compiler_params=pltpu.CompilerParams(
            collective_id=0, has_side_effects=True, vmem_limit_bytes=60 * 2**20
        ),
        name="back_transform",
    )(block_start, panel, cauchy, refl_v)


def solution(mesh):
    placed = (P("col", "row"), P(), P(None, "row", None, None), P())
    return jax.shard_map(
        shards, mesh=mesh, in_specs=placed, out_specs=P("col", "row"), check_vma=False
    )
```

time: 69 us -> 55.2 us (0.80)
  Pallas kernels: 66.6 us -> 53.1 us
    pallas_call x1, Pallas kernels: 66.6 us -> 53.1 us  [shards(): pl.pallas_call(functools.partial(kernel, inner), in_specs=[SMEM, ANY, VME...]
where the time goes in v1:
time: 55.2 us; the launch traced here: 55 us
  Pallas kernels  53.1 us (96%)
  local copies, waits for them, and re-layouts  1.87 us (3%)
    pallas_call x1, Pallas kernels, shards(): pl.pallas_call(functools.partial(kernel, inner), in_specs=[SMEM, ANY, VME...  53.1 us
    unnamed x1, local copies, waits for them, and re-layouts  1.87 us

profile of v1, /device:TPU:1, one launch (start us, length us, event | category | flops | bytes accessed | tf_op | source)
XLA Modules:
  0.0 55.0 jit_solution(10705740847047961126)
XLA Ops:
  0.0 53.1 %back_transform.1 = f32[64,2048]{1,0:T(8,128)} custom-call(s32[2]{0:T(128)} %offset_ref.1, f32[64,2048]{1,0:T(8,128)} %panel_ref.1, f32[256,256]{1,0:T(8,128)} %cauchy_ref.1, f32[2,16,256,128]{3,2,1,0:T(8,128)} %v_ref.1), custom_call_target="tpu_custom_call" | custom-call | tf_op jit(solution)/shard_map/back_transform/pallas_call | solution.py:635
  53.1 1.9 %copy.6 = f32[64,2048]{1,0:T(8,128)} copy(f32[64,2048]{1,0:T(8,128)} %back_transform.1) | data formatting | bytes 1048576

commit v2 on v1

--- a/solution.py
+++ b/solution.py
@@ -12,7 +12,7 @@
 MESH = pl.DeviceIdType.MESH
 VMEM = pl.BlockSpec(memory_space=pltpu.VMEM)
 SMEM = pl.BlockSpec(memory_space=pltpu.SMEM)
-ANY = pl.BlockSpec(memory_space=pl.ANY)
+HBM = pl.BlockSpec(memory_space=pltpu.HBM)
 
 
 def split(x):
@@ -151,7 +151,7 @@
 
 def kernel(
     inner, offset_ref, panel_ref, cauchy_ref, v_ref, out_ref,
-    v_all, k_high, k_low, panels, turned, home, mid_map, mid_data, z_high, z_low, aligned,
+    v_all, k_high, k_low, panels, mixing, turned, home, mid_map, mid_data, z_all, z_high, z_low, aligned, y_home,
     map_one, map_two, data_one, data_two,
     pair_m, chip_m, chips_m, layer_m, layers_m, own_b, pair_b, chip_b, chips_b, layer_b, layers_b,
     own_m, ready_s, ready_r, load_sem, ring_send, ring_sem, halo_send, halo_sem, scan_send, scan_sem,
@@ -183,6 +183,7 @@
             )
         )
     loads.append(pltpu.make_async_copy(panel_ref, panels.at[col], load_sem.at[4]))
+    loads.append(pltpu.make_async_copy(cauchy_ref, mixing, load_sem.at[5]))
     loads[0].start()
 
     barrier = pltpu.get_barrier_semaphore()
@@ -383,7 +384,7 @@
         at = k + steps + 4
         x = jnp.concatenate([map_two[...], jnp.concatenate([fresh, zero], axis=0)], axis=1)
         out = mul(x, k_high[at], k_low[at])
-        z_high[k + 1], z_low[k + 1] = split(out[:, :S])
+        z_all[k + 1] = out[:, :S]
         map_two[...] = out[:, S:]
 
     def wave(k, one, two, save_one, save_two):
@@ -440,7 +441,8 @@
     for copy in halos:
         copy.wait()
     begin(seam, ends(batch_of(steps // 4 - 1)))
-    turned[...] = cauchy_ref[...].T
+    loads[5].wait()
+    turned[...] = mixing[...].T
     mix_high, mix_low = split(turned[pl.ds(pl.multiple_of(col * rows, rows), rows)])
     mix = jnp.concatenate([mix_high, mix_low], axis=0)
     home[0] = jnp.zeros((rows, S), F32)
@@ -497,13 +499,15 @@
     pair = send(own_m, pair_m, scan_send.at[0], scan_sem.at[0], {"row": partner})
     pair.start()
 
-    pair.wait()
     on_first = core == 0
-    first_m = jnp.where(on_first, whole(own_m), whole(pair_m))
-    second_m = jnp.where(on_first, whole(pair_m), whole(own_m))
-    keep(chip_m, mul(first_m, *split(second_m)))
-    chip_ring_m.start()
-    chips_m[chip] = chip_m[...]
+
+    def pair_maps():
+        pair.wait()
+        first = jnp.where(on_first, whole(own_m), whole(pair_m))
+        second = jnp.where(on_first, whole(pair_m), whole(own_m))
+        keep(chip_m, mul(first, *split(second)))
+        chip_ring_m.start()
+        chips_m[chip] = chip_m[...]
 
     def fresh_one(k):
         return window(home[k + 1], home[k + 2], o_one)
@@ -545,17 +549,26 @@
             margin.wait_recv()
 
     also = {
-        4: merge_second, 7: chip_ring_m.forward, 11: chip_ring_m.swap_near, steps - 2: take_margin,
-        steps + 1: chip_ring_m.swap_far,
+        3: pair_maps, 5: merge_second, 12: chip_ring_m.forward, steps - 2: take_margin,
+        steps: chip_ring_m.swap_near,
     }
     for k in range(-1, steps + 3):
         if k in also:
             also[k]()
         wave(k, data_step_one, data_step_two, save_data_one, save_data_two)
 
-    pair = send(own_b, pair_b, scan_send.at[1], scan_sem.at[1], {"row": partner})
-    pair.start()
-
+    pair_two = send(own_b, pair_b, scan_send.at[1], scan_sem.at[1], {"row": partner})
+    pair_two.start()
+
+    chip_ring_m.swap_far()
+    pair_two.wait()
+    first_m = jnp.where(on_first, whole(own_m), whole(pair_m))
+    second_m = jnp.where(on_first, whole(pair_m), whole(own_m))
+    first_b = jnp.where(on_first, own_b[...], pair_b[...])
+    second_b = jnp.where(on_first, pair_b[...], own_b[...])
+    chip_b[...] = mul(first_b, *split(second_m)) + second_b
+    chip_ring_b.start()
+    chips_b[chip] = chip_b[...]
     chip_ring_m.arrive()
     total = whole(chips_m.at[0])
     lead = eye2
@@ -565,17 +578,16 @@
     keep(layer_m, total)
     layer_ring_m.start()
     layers_m[layer] = layer_m[...]
-
-    pair.wait()
-    first_b = jnp.where(on_first, own_b[...], pair_b[...])
-    second_b = jnp.where(on_first, pair_b[...], own_b[...])
-    chip_b[...] = mul(first_b, *split(second_m)) + second_b
-    chip_ring_b.start()
-    chips_b[chip] = chip_b[...]
     lead_m = jnp.where(on_first, lead, mul(lead, *split(first_m)))
     chip_ring_b.relay()
     layer_ring_m.forward()
-    layer_ring_m.swap_near()
+    reach_out = S - o_two
+    jump_out = reach_out // S
+    by_out = lax.rem(reach_out, S)
+
+    for j in range(steps):
+        y_home[:, j * S : (j + 1) * S] = window(aligned[j + jump_out], aligned[j + jump_out + 1], by_out)
+        z_high[j], z_low[j] = split(window(z_all[j + jump_out], z_all[j + jump_out + 1], by_out))
     chip_ring_b.arrive()
     total_b = chips_b[0]
     lead_b = jnp.zeros((rows, 2 * S), F32)
@@ -586,28 +598,19 @@
     layer_ring_b.start()
     layers_b[layer] = layer_b[...]
     lead_b = jnp.where(on_first, lead_b, mul(lead_b, *split(first_m)) + first_b)
+    layer_ring_m.swap_near()
     layer_ring_m.swap_far()
     layer_ring_b.relay()
     layer_ring_m.arrive()
     layer_ring_b.arrive()
-    carry = jnp.zeros((rows, 2 * S), F32)
-    for z in range(outer - 1):
+    carry = jnp.where(layer > 0, layers_b[0], 0.0)
+    for z in range(1, outer - 1):
         longer = mul(carry, *matrix(layers_m.at[z])) + layers_b[z]
         carry = jnp.where(z < layer, longer, carry)
     carry = mul(carry, *split(lead_m)) + lead_b
-
-    high, low = split(carry)
-    both = jnp.concatenate([high, low], axis=0)
-    for j in range(steps + 1):
-        part = dot(both, z_high[j])
-        aligned[j] = aligned[j] + (part[:rows] + (part[rows:] + dot(high, z_low[j])))
-    reach_out = S - o_two
-    jump_out = reach_out // S
-    by_out = lax.rem(reach_out, S)
     for j in range(steps):
-        out_ref[:, j * S : (j + 1) * S] = window(
-            aligned[j + jump_out], aligned[j + jump_out + 1], by_out
-        )
+        here = slice(j * S, (j + 1) * S)
+        out_ref[:, here] = y_home[:, here] + mul(carry, z_high[j], z_low[j])
     for ring in (*panel_rings, chip_ring_m, chip_ring_b, layer_ring_m, layer_ring_b):
         ring.finish()
 
@@ -634,20 +637,20 @@
     dma = pltpu.SemaphoreType.DMA
     return pl.pallas_call(
         functools.partial(kernel, inner),
-        in_specs=[SMEM, ANY, VMEM, ANY],
+        in_specs=[SMEM, HBM, HBM, HBM],
         out_specs=VMEM,
-        out_shape=jax.ShapeDtypeStruct((rows, width), F32),
+        out_shape=pltpu.VMEM((rows, width), F32),
         scratch_shapes=[
             f(count, 2 * S, S), b(count, 2 * S, 2 * S), b(count, 2 * S, 2 * S),
-            f(cols, rows, width), f(2 * S, 2 * S), f(steps + 5, rows, S),
+            f(cols, rows, width), f(2 * S, 2 * S), f(2 * S, 2 * S), f(steps + 5, rows, S),
             f(steps + 5, S, S), f(steps + 5, rows, S),
-            b(steps + 1, 2 * S, S), b(steps + 1, 2 * S, S), f(steps + 2, rows, S),
+            f(steps + 2, 2 * S, S), b(steps, 2 * S, S), b(steps, 2 * S, S), f(steps + 2, rows, S), f(rows, width),
             f(S, S), f(2 * S, S), f(rows, S), f(rows, S),
             f(3, S, S), f(3, S, S), f(inner, 3, S, S), f(3, S, S), f(outer, 3, S, S),
             f(rows, 2 * S), f(rows, 2 * S), f(rows, 2 * S), f(inner, rows, 2 * S),
             f(rows, 2 * S), f(outer, rows, 2 * S), f(3, S, S),
             f(8, 8, S), f(8, S, S),
-            dma((5,)), dma((12,)), dma((12,)), dma((4,)), dma((4,)),
+            dma((6,)), dma((12,)), dma((12,)), dma((4,)), dma((4,)),
             dma((scan_copies,)), dma((scan_copies,)),
         ],
         compiler_params=pltpu.CompilerParams(
@@ -656,7 +659,6 @@
         name="back_transform",
     )(block_start, panel, cauchy, refl_v)
 
-
 def solution(mesh):
     placed = (P("col", "row"), P(), P(None, "row", None, None), P())
     return jax.shard_map(

time: 55.2 us -> 52.7 us (0.955)
  Pallas kernels: 53.1 us -> 51.7 us
  local copies, waits for them, and re-layouts: 1.87 us -> 0.8 us
    pallas_call x1, Pallas kernels: 53.1 us -> 51.7 us  [shards(): pl.pallas_call(functools.partial(kernel, inner), in_specs=[SMEM, HBM, HBM...]
    unnamed x1, local copies, waits for them, and re-layouts: 1.87 us -> 0.8 us
where the time goes in v2:
time: 52.7 us; the launch traced here: 52.5 us
  Pallas kernels  51.7 us (98%)
  local copies, waits for them, and re-layouts  0.8 us (2%)
    pallas_call x1, Pallas kernels, shards(): pl.pallas_call(functools.partial(kernel, inner), in_specs=[SMEM, HBM, HBM...  51.7 us

profile of v2, /device:TPU:1, one launch (start us, length us, event | category | flops | bytes accessed | tf_op | source)
XLA Modules:
  0.0 52.5 jit_solution(16671222182870204666)
XLA Ops:
  0.0 51.7 %back_transform.1 = f32[64,2048]{1,0:T(8,128)S(1)} custom-call(s32[2]{0:T(128)} %offset_ref.1, f32[64,2048]{1,0:T(8,128)} %panel_ref.1, f32[256,256]{1,0:T(8,128)} %cauchy_ref.1, f32[2,16,256,128]{3,2,1,0:T(8,128)} %v_ref.1), custom_call_target="tpu_custom_call" | custom-call | tf_op jit(solution)/shard_map/back_transform/pallas_call | solution.py:638
  51.7 0.8 %copy.6 = f32[64,2048]{1,0:T(8,128)} copy(f32[64,2048]{1,0:T(8,128)S(1)} %back_transform.1) | data formatting | bytes 1048576

commit v3 on v2

--- a/solution.py
+++ b/solution.py
@@ -189,7 +189,9 @@
     barrier = pltpu.get_barrier_semaphore()
     for peer in (right, left):
         pl.semaphore_signal(barrier, inc=1, device_id={"col": peer}, device_id_type=MESH)
-    for peer in [after, before, partner] + near + apart:
+    sides = [near[0], near[-1]]
+    greeted = [after, before, partner] + near + apart + [peer + 1 - 2 * core for peer in sides]
+    for peer in greeted:
         pl.semaphore_signal(barrier, inc=1, device_id={"row": peer}, device_id_type=MESH)
 
     def send(source, target, send_sem, recv_sem, device):
@@ -240,17 +242,35 @@
                 copy.wait_send()
 
     class SplitRing(Ring):
-        def __init__(self, source, slots, place, size, axis, peer, send_sem, recv_sem, base):
+        def __init__(self, source, slots, place, size, axis, peer, send_sem, recv_sem, base, cross):
             at, quarter = core * (S // 2), S // 4
             parts = [(slice(None), pl.ds(pl.multiple_of(at + i * quarter, quarter), quarter)) for i in range(2)]
             super().__init__(source, slots, place, size, axis, peer, parts, send_sem, recv_sem, base)
             rows_here = pl.ds(pl.multiple_of(at, S // 2), S // 2)
-            self.swaps = []
-            for i, shift in enumerate((size - 1, 1, 2)):
+            across = 1 - 2 * core
+            self.swaps, self.crossed = [], []
+            for i, shift in enumerate((size - 1, 1)):
                 ref = slots.at[lax.rem(place + shift, size), :, rows_here]
                 self.swaps.append(
                     send(ref, ref, send_sem.at[base + 6 + i], recv_sem.at[base + 6 + i], {"row": partner})
                 )
+                if cross:
+                    ref = slots.at[(lax.rem(place + shift, size), *parts[i])]
+                    other = peer(lax.rem(place + size - shift, size)) + across
+                    self.crossed.append(
+                        send(ref, ref, send_sem.at[base + 8 + i], recv_sem.at[base + 8 + i], {axis: other})
+                    )
+            if not cross:
+                ref = slots.at[lax.rem(place + 2, size), :, rows_here]
+                self.far = send(ref, ref, send_sem.at[base + 8], recv_sem.at[base + 8], {"row": partner})
+                self.swaps.append(self.far)
+
+        def forward(self):
+            for i in range(2):
+                self.first[i].wait_recv()
+                self.second[i].start()
+                if self.crossed:
+                    self.crossed[i].start()
 
         def swap_near(self):
             for copy, swap in zip(self.first[2:], self.swaps):
@@ -260,14 +280,14 @@
         def swap_far(self):
             for copy in self.second:
                 copy.wait_recv()
-            self.swaps[2].start()
+            self.far.start()
 
         def arrive(self):
-            for swap in self.swaps:
-                swap.wait_recv()
+            for copy in self.swaps + (self.second + self.crossed if self.crossed else []):
+                copy.wait_recv()
 
         def finish(self):
-            for copy in self.first + self.second + self.swaps:
+            for copy in self.first + self.second + self.swaps + self.crossed:
                 copy.wait_send()
 
     class Direct:
@@ -310,10 +330,10 @@
     over_layers = dict(place=layer, size=outer, axis="row", peer=lambda z: z * group + 2 * chip + core)
 
     scan_sems = dict(send_sem=scan_send, recv_sem=scan_sem)
-    chip_ring_m = SplitRing(chip_m, chips_m, base=2, **in_layer, **scan_sems)
-    layer_ring_m = SplitRing(layer_m, layers_m, base=11, **over_layers, **scan_sems)
-    chip_ring_b = Direct(chip_b, chips_b, base=20, **in_layer, **scan_sems)
-    layer_ring_b = Direct(layer_b, layers_b, base=24, **over_layers, **scan_sems)
+    chip_ring_m = SplitRing(chip_m, chips_m, base=2, cross=True, **in_layer, **scan_sems)
+    layer_ring_m = SplitRing(layer_m, layers_m, base=12, cross=False, **over_layers, **scan_sems)
+    chip_ring_b = Direct(chip_b, chips_b, base=22, **in_layer, **scan_sems)
+    layer_ring_b = Direct(layer_b, layers_b, base=26, **over_layers, **scan_sems)
 
     last = slabs * steps - 3
     row = lax.broadcasted_iota(jnp.int32, (2 * S, 2 * S), 0)
@@ -415,7 +435,7 @@
         return out
 
     def enter():
-        pl.semaphore_wait(barrier, 5 + len(near) + len(apart))
+        pl.semaphore_wait(barrier, 2 + len(greeted))
         for copy in halos:
             copy.start()
         panel_rings[0].start()
@@ -463,23 +483,20 @@
         panel_rings[0].arrive()
         lax.fori_loop(0, steps // 2, merge, 0, unroll=4)
 
-        @pl.when(me > 0)
-        def _():
-            margin.start()
-
         @pl.when(me == slabs - 1)
         def _():
             home[pl.ds(steps + 1, 4)] = jnp.zeros((4, rows, S), F32)
 
 
-    for piece in ends(seam):
-        piece()
-    merge_first()
-    for piece in map_waves(range(-1, 9)):
+    for piece in ends(seam) + map_waves(range(-1, 9)):
         piece()
     panel_rings[1].forward()
-    for piece in map_waves(range(9, steps + 3)):
+    for piece in map_waves(range(9, steps + 2)):
         piece()
+    pair = send(own_m, pair_m, scan_send.at[0], scan_sem.at[0], {"row": partner})
+    pair.start()
+    map_waves([steps + 2])[0]()
+    merge_first()
 
     def matrix(ref):
         high0, low0 = split(jnp.concatenate([ref[0], ref[1]], axis=1))
@@ -495,9 +512,6 @@
         ref[0] = x[:S, :S]
         ref[1] = x[:S, S:]
         ref[2] = x[S:, S:]
-
-    pair = send(own_m, pair_m, scan_send.at[0], scan_sem.at[0], {"row": partner})
-    pair.start()
 
     on_first = core == 0
 
@@ -507,6 +521,11 @@
         second = jnp.where(on_first, whole(pair_m), whole(own_m))
         keep(chip_m, mul(first, *split(second)))
         chip_ring_m.start()
+
+        @pl.when(me > 0)
+        def _():
+            margin.start()
+
         chips_m[chip] = chip_m[...]
 
     def fresh_one(k):
@@ -548,19 +567,19 @@
         def _():
             margin.wait_recv()
 
+    pair_two = send(own_b, pair_b, scan_send.at[1], scan_sem.at[1], {"row": partner})
     also = {
-        3: pair_maps, 5: merge_second, 12: chip_ring_m.forward, steps - 2: take_margin,
+        0: pair_maps, 5: merge_second, 12: chip_ring_m.forward, steps - 2: take_margin,
         steps: chip_ring_m.swap_near,
     }
     for k in range(-1, steps + 3):
         if k in also:
             also[k]()
         wave(k, data_step_one, data_step_two, save_data_one, save_data_two)
-
-    pair_two = send(own_b, pair_b, scan_send.at[1], scan_sem.at[1], {"row": partner})
-    pair_two.start()
-
-    chip_ring_m.swap_far()
+        if k == steps + 1:
+            pair_two.start()
+
+
     pair_two.wait()
     first_m = jnp.where(on_first, whole(own_m), whole(pair_m))
     second_m = jnp.where(on_first, whole(pair_m), whole(own_m))
@@ -570,17 +589,27 @@
     chip_ring_b.start()
     chips_b[chip] = chip_b[...]
     chip_ring_m.arrive()
-    total = whole(chips_m.at[0])
-    lead = eye2
-    for j in range(1, inner):
-        lead = jnp.where(chip == j, total, lead)
-        total = mul(total, *matrix(chips_m.at[j]))
-    keep(layer_m, total)
+    pieces = [whole(chips_m.at[j]) for j in range(inner)]
+    halves = [split(x) for x in pieces]
+    early = mul(pieces[0], *halves[1])
+    late = mul(pieces[2], *halves[3])
+    late_parts = split(late)
+    keep(layer_m, mul(early, *late_parts))
     layer_ring_m.start()
     layers_m[layer] = layer_m[...]
+    lead = jnp.where(chip == 0, eye2, jnp.where(chip == 1, pieces[0], early))
+    lead = jnp.where(chip == 3, mul(early, *halves[2]), lead)
     lead_m = jnp.where(on_first, lead, mul(lead, *split(first_m)))
     chip_ring_b.relay()
     layer_ring_m.forward()
+    chip_ring_b.arrive()
+    early_b = mul(chips_b[0], *halves[1]) + chips_b[1]
+    layer_b[...] = mul(early_b, *late_parts) + (mul(chips_b[2], *halves[3]) + chips_b[3])
+    layer_ring_b.start()
+    layers_b[layer] = layer_b[...]
+    lead_b = jnp.where(chip == 0, 0.0, jnp.where(chip == 1, chips_b[0], early_b))
+    lead_b = jnp.where(chip == 3, mul(early_b, *halves[2]) + chips_b[2], lead_b)
+    lead_b = jnp.where(on_first, lead_b, mul(lead_b, *split(first_m)) + first_b)
     reach_out = S - o_two
     jump_out = reach_out // S
     by_out = lax.rem(reach_out, S)
@@ -588,16 +617,6 @@
     for j in range(steps):
         y_home[:, j * S : (j + 1) * S] = window(aligned[j + jump_out], aligned[j + jump_out + 1], by_out)
         z_high[j], z_low[j] = split(window(z_all[j + jump_out], z_all[j + jump_out + 1], by_out))
-    chip_ring_b.arrive()
-    total_b = chips_b[0]
-    lead_b = jnp.zeros((rows, 2 * S), F32)
-    for j in range(1, inner):
-        lead_b = jnp.where(chip == j, total_b, lead_b)
-        total_b = mul(total_b, *matrix(chips_m.at[j])) + chips_b[j]
-    layer_b[...] = total_b
-    layer_ring_b.start()
-    layers_b[layer] = layer_b[...]
-    lead_b = jnp.where(on_first, lead_b, mul(lead_b, *split(first_m)) + first_b)
     layer_ring_m.swap_near()
     layer_ring_m.swap_far()
     layer_ring_b.relay()
@@ -626,7 +645,7 @@
     inner = 4
     outer = slabs // (2 * inner)
     count = 2 * steps + 4
-    scan_copies = 2 + 2 * 9 + 2 * 4
+    scan_copies = 2 + 2 * 10 + 2 * 4
 
     def f(*shape):
         return pltpu.VMEM(shape, F32)

time: 52.7 us -> 50.6 us (0.960)
  Pallas kernels: 51.7 us -> 49.6 us
    pallas_call x1, Pallas kernels: 51.7 us -> 49.6 us  [shards(): pl.pallas_call(functools.partial(kernel, inner), in_specs=[SMEM, HBM, HBM...]
where the time goes in v3:
time: 50.6 us; the launch traced here: 50.4 us
  Pallas kernels  49.6 us (98%)
  local copies, waits for them, and re-layouts  0.8 us (2%)
    pallas_call x1, Pallas kernels, shards(): pl.pallas_call(functools.partial(kernel, inner), in_specs=[SMEM, HBM, HBM...  49.6 us

profile of v3, /device:TPU:1, one launch (start us, length us, event | category | flops | bytes accessed | tf_op | source)
XLA Modules:
  0.0 50.4 jit_solution(16781357888956207501)
XLA Ops:
  0.0 49.6 %back_transform.1 = f32[64,2048]{1,0:T(8,128)S(1)} custom-call(s32[2]{0:T(128)} %offset_ref.1, f32[64,2048]{1,0:T(8,128)} %panel_ref.1, f32[256,256]{1,0:T(8,128)} %cauchy_ref.1, f32[2,16,256,128]{3,2,1,0:T(8,128)} %v_ref.1), custom_call_target="tpu_custom_call" | custom-call | tf_op jit(solution)/shard_map/back_transform/pallas_call | solution.py:657
  49.7 0.8 %copy.6 = f32[64,2048]{1,0:T(8,128)} copy(f32[64,2048]{1,0:T(8,128)S(1)} %back_transform.1) | data formatting | bytes 1048576

commit v4 on v3

--- a/solution.py
+++ b/solution.py
@@ -120,23 +120,24 @@
 def prepare(blocks, active):
     row = lax.broadcasted_iota(jnp.int32, (S, S), 0)
     col = lax.broadcasted_iota(jnp.int32, (S, S), 1)
-    eye = (row == col).astype(F32)
-    quads = [dot(v.T.astype(BF), wide(v)) for v in blocks]
+    pairs = [wide(v) for v in blocks]
+    quads = [dot(v.T.astype(BF), p) for v, p in zip(blocks, pairs)]
     yield
     grams = [fold(q) + q[:, S:].T for q in quads]
     scale = [
-        jnp.where(on, -2.0 / jnp.sum(g * eye, axis=0, keepdims=True), 0.0)
-        for g, on in zip(grams, active)
+        jnp.where(on, -2.0 / jnp.sum(v * v, axis=0, keepdims=True), 0.0)
+        for v, on in zip(blocks, active)
     ]
     nils = [jnp.where(row > col, g * -s, 0.0) for g, s in zip(grams, scale)]
     yield
     result = yield from unit_inverses(nils)
-    return scale, result
-
-
-def less(v, scale, result):
-    high, low = split(fold(dot(wide(v * scale), square(result))))
-    v_high, v_low = split(v)
+    result = [jnp.broadcast_to(s, (S, S)).T * r for s, r in zip(scale, result)]
+    return pairs, result
+
+
+def less(v_pair, result):
+    high, low = split(fold(dot(v_pair, square(result))))
+    v_high, v_low = v_pair[:, :S], v_pair[:, S:]
     both = jnp.concatenate([high, low], axis=1)
     return dot_t(both, jnp.concatenate([v_high, v_high], axis=1)) + dot_t(high, v_low)
 
@@ -154,7 +155,7 @@
     v_all, k_high, k_low, panels, mixing, turned, home, mid_map, mid_data, z_all, z_high, z_low, aligned, y_home,
     map_one, map_two, data_one, data_two,
     pair_m, chip_m, chips_m, layer_m, layers_m, own_b, pair_b, chip_b, chips_b, layer_b, layers_b,
-    own_m, ready_s, ready_r, load_sem, ring_send, ring_sem, halo_send, halo_sem, scan_send, scan_sem,
+    own_m, ready_v, ready_r, load_sem, ring_send, ring_sem, halo_send, halo_sem, scan_send, scan_sem,
 ):
     me, slabs = lax.axis_index("row"), lax.axis_size("row")
     col, cols = lax.axis_index("col"), lax.axis_size("col")
@@ -184,7 +185,12 @@
         )
     loads.append(pltpu.make_async_copy(panel_ref, panels.at[col], load_sem.at[4]))
     loads.append(pltpu.make_async_copy(cauchy_ref, mixing, load_sem.at[5]))
-    loads[0].start()
+    head_loads = []
+    for i in range(4):
+        head_loads.append(
+            pltpu.make_async_copy(v_ref.at[0, pl.ds(2 * i, 2)], v_all.at[pl.ds(1 + 2 * i, 2)], load_sem.at[6 + i])
+        )
+        head_loads[-1].start()
 
     barrier = pltpu.get_barrier_semaphore()
     for peer in (right, left):
@@ -351,7 +357,7 @@
             try:
                 next(stages)
             except StopIteration as done:
-                scale, result = done.value
+                pairs, result = done.value
                 break
             for piece in filler[:share]:
                 piece()
@@ -359,11 +365,11 @@
         for piece in filler:
             piece()
         for i in range(len(batch)):
-            ready_s[i] = jnp.broadcast_to(scale[i], (8, S))
+            ready_v[i] = pairs[i]
             ready_r[i] = result[i]
 
     def end(i, at):
-        x = less(v_all[at], ready_s[i, :1], ready_r[i])
+        x = less(ready_v[i], ready_r[i])
         for r in range(2):
             for c in range(2):
                 here = pl.ds(r * S, S), pl.ds(c * S, S)
@@ -440,7 +446,8 @@
             copy.start()
         panel_rings[0].start()
 
-    loads[0].wait()
+    for copy in head_loads:
+        copy.wait()
     for copy in loads[1:]:
         copy.start()
     begin(batch_of(0), [])
@@ -560,7 +567,7 @@
 
     def merge_second():
         panel_rings[1].arrive()
-        lax.fori_loop(steps // 2, steps, merge, 0, unroll=4)
+        lax.fori_loop(steps // 2, steps, merge, 0, unroll=True)
 
     def take_margin():
         @pl.when(me < slabs - 1)
@@ -668,8 +675,8 @@
             f(3, S, S), f(3, S, S), f(inner, 3, S, S), f(3, S, S), f(outer, 3, S, S),
             f(rows, 2 * S), f(rows, 2 * S), f(rows, 2 * S), f(inner, rows, 2 * S),
             f(rows, 2 * S), f(outer, rows, 2 * S), f(3, S, S),
-            f(8, 8, S), f(8, S, S),
-            dma((6,)), dma((12,)), dma((12,)), dma((4,)), dma((4,)),
+            b(8, 2 * S, 2 * S), f(8, S, S),
+            dma((10,)), dma((12,)), dma((12,)), dma((4,)), dma((4,)),
             dma((scan_copies,)), dma((scan_copies,)),
         ],
         compiler_params=pltpu.CompilerParams(

time: 50.6 us -> 50.7 us (level)
  no operation moved by 1% of the time
where the time goes in v4:
time: 50.7 us; the launch traced here: 50.5 us
  Pallas kernels  49.7 us (98%)
  local copies, waits for them, and re-layouts  0.8 us (2%)
    pallas_call x1, Pallas kernels, shards(): pl.pallas_call(functools.partial(kernel, inner), in_specs=[SMEM, HBM, HBM...  49.7 us

profile of v4, /device:TPU:1, one launch (start us, length us, event | category | flops | bytes accessed | tf_op | source)
XLA Modules:
  0.0 50.5 jit_solution(13788560189695212622)
XLA Ops:
  0.0 49.7 %back_transform.1 = f32[64,2048]{1,0:T(8,128)S(1)} custom-call(s32[2]{0:T(128)} %offset_ref.1, f32[64,2048]{1,0:T(8,128)} %panel_ref.1, f32[256,256]{1,0:T(8,128)} %cauchy_ref.1, f32[2,16,256,128]{3,2,1,0:T(8,128)} %v_ref.1), custom_call_target="tpu_custom_call" | custom-call | tf_op jit(solution)/shard_map/back_transform/pallas_call | solution.py:664
  49.7 0.8 %copy.6 = f32[64,2048]{1,0:T(8,128)} copy(f32[64,2048]{1,0:T(8,128)S(1)} %back_transform.1) | data formatting | bytes 1048576

commit v5 on v4

--- a/solution.py
+++ b/solution.py
@@ -296,8 +296,51 @@
             for copy in self.first + self.second + self.swaps + self.crossed:
                 copy.wait_send()
 
+    def only(on, act):
+        if on is None:
+            act()
+        elif on is not False:
+            pl.when(on)(act)
+
+    z1, z2 = layer == 1, layer == 2
+    upper, top_layer, bottom = layer > 1, layer == outer - 1, layer == 0
+
+    class LayerMaps(SplitRing):
+        def start(self):
+            self.first, self.sent = self.first[:3], [z1 | z2, z1, z1 | z2]
+            for copy, on in zip(self.first, self.sent):
+                only(on, copy.start)
+
+        def forward(self):
+            for i, (came, here) in enumerate([(upper, z2), (bottom, bottom)]):
+                only(came, self.first[i].wait_recv)
+                only(here, self.second[i].start)
+
+        def swap_near(self):
+            only(upper, self.first[2].wait_recv)
+            only(upper, self.swaps[0].start)
+
+        def swap_far(self):
+            for copy in self.second:
+                only(top_layer, copy.wait_recv)
+            only(top_layer, self.far.start)
+
+        def arrive(self):
+            only(upper, self.swaps[0].wait_recv)
+            only(top_layer, self.far.wait_recv)
+
+        def finish(self):
+            for copy, on in zip(self.first, self.sent):
+                only(on, copy.wait_send)
+            only(z2, self.second[0].wait_send)
+            only(bottom, self.second[1].wait_send)
+            only(upper, self.swaps[0].wait_send)
+            only(top_layer, self.far.wait_send)
+
     class Direct:
-        def __init__(self, source, slots, place, size, axis, peer, send_sem, recv_sem, base):
+        def __init__(self, source, slots, place, size, axis, peer, send_sem, recv_sem, base, later):
+            self.sends = [place < size - 2, place < size - 1, place == 0] if later else [None] * 3
+            self.comes = [place > 1, place > 0, place == size - 1] if later else [None] * 3
             mine = pl.ds(pl.multiple_of(core * half, half), half)
             to = [{axis: peer(lax.rem(place + shift, size))} for shift in (2, 1, size - 1)]
             refs = [(source.at[mine], slots.at[place, mine])] + [(source, slots.at[place])] * 2
@@ -309,20 +352,20 @@
             self.swap = send(ref, ref, send_sem.at[base + 3], recv_sem.at[base + 3], {"row": partner})
 
         def start(self):
-            for copy in self.copies:
-                copy.start()
+            for copy, on in zip(self.copies, self.sends):
+                only(on, copy.start)
 
         def relay(self):
-            self.copies[0].wait_recv()
-            self.swap.start()
+            only(self.comes[0], self.copies[0].wait_recv)
+            only(self.comes[0], self.swap.start)
 
         def arrive(self):
-            for copy in [*self.copies[1:], self.swap]:
-                copy.wait_recv()
+            for copy, on in zip([*self.copies[1:], self.swap], [*self.comes[1:], self.comes[0]]):
+                only(on, copy.wait_recv)
 
         def finish(self):
-            for copy in [*self.copies, self.swap]:
-                copy.wait_send()
+            for copy, on in zip([*self.copies, self.swap], [*self.sends, self.comes[0]]):
+                only(on, copy.wait_send)
 
     flat = [(pl.ds(i * half, half),) for i in range(2)]
     width = panel_ref.shape[1] // 2
@@ -337,9 +380,9 @@
 
     scan_sems = dict(send_sem=scan_send, recv_sem=scan_sem)
     chip_ring_m = SplitRing(chip_m, chips_m, base=2, cross=True, **in_layer, **scan_sems)
-    layer_ring_m = SplitRing(layer_m, layers_m, base=12, cross=False, **over_layers, **scan_sems)
-    chip_ring_b = Direct(chip_b, chips_b, base=22, **in_layer, **scan_sems)
-    layer_ring_b = Direct(layer_b, layers_b, base=26, **over_layers, **scan_sems)
+    layer_ring_m = LayerMaps(layer_m, layers_m, base=12, cross=False, **over_layers, **scan_sems)
+    chip_ring_b = Direct(chip_b, chips_b, base=22, later=False, **in_layer, **scan_sems)
+    layer_ring_b = Direct(layer_b, layers_b, base=26, later=True, **over_layers, **scan_sems)
 
     last = slabs * steps - 3
     row = lax.broadcasted_iota(jnp.int32, (2 * S, 2 * S), 0)

time: 50.7 us -> 46.8 us (0.923); the launches traced: 50.5 us -> 46.1 us
  Pallas kernels: 49.7 us -> 45.3 us
    pallas_call x1, Pallas kernels: 49.7 us -> 45.3 us  [shards(): pl.pallas_call(functools.partial(kernel, inner), in_specs=[SMEM, HBM, HBM...]
where the time goes in v5:
time: 46.8 us; the launch traced here: 46.1 us
  Pallas kernels  45.3 us (97%)
  local copies, waits for them, and re-layouts  0.8 us (2%)
    pallas_call x1, Pallas kernels, shards(): pl.pallas_call(functools.partial(kernel, inner), in_specs=[SMEM, HBM, HBM...  45.3 us

profile of v5, /device:TPU:1, one launch (start us, length us, event | category | flops | bytes accessed | tf_op | source)
XLA Modules:
  0.0 46.1 jit_solution(13836592516011203372)
XLA Ops:
  0.0 45.3 %back_transform.1 = f32[64,2048]{1,0:T(8,128)S(1)} custom-call(s32[2]{0:T(128)} %offset_ref.1, f32[64,2048]{1,0:T(8,128)} %panel_ref.1, f32[256,256]{1,0:T(8,128)} %cauchy_ref.1, f32[2,16,256,128]{3,2,1,0:T(8,128)} %v_ref.1), custom_call_target="tpu_custom_call" | custom-call | tf_op jit(solution)/shard_map/back_transform/pallas_call | solution.py:707
  45.3 0.8 %copy.6 = f32[64,2048]{1,0:T(8,128)} copy(f32[64,2048]{1,0:T(8,128)S(1)} %back_transform.1) | data formatting | bytes 1048576

commit v6 on v5

--- a/solution.py
+++ b/solution.py
@@ -312,9 +312,12 @@
                 only(on, copy.start)
 
         def forward(self):
-            for i, (came, here) in enumerate([(upper, z2), (bottom, bottom)]):
-                only(came, self.first[i].wait_recv)
-                only(here, self.second[i].start)
+            only(upper, self.first[0].wait_recv)
+            only(z2, self.second[0].start)
+
+        def forward_down(self):
+            only(bottom, self.first[1].wait_recv)
+            only(bottom, self.second[1].start)
 
         def swap_near(self):
             only(upper, self.first[2].wait_recv)
@@ -656,6 +659,7 @@
     early_b = mul(chips_b[0], *halves[1]) + chips_b[1]
     layer_b[...] = mul(early_b, *late_parts) + (mul(chips_b[2], *halves[3]) + chips_b[3])
     layer_ring_b.start()
+    layer_ring_m.forward_down()
     layers_b[layer] = layer_b[...]
     lead_b = jnp.where(chip == 0, 0.0, jnp.where(chip == 1, chips_b[0], early_b))
     lead_b = jnp.where(chip == 3, mul(early_b, *halves[2]) + chips_b[2], lead_b)

time: 46.8 us -> 47.7 us (1.019)
  the two profiles are of different devices: /device:TPU:1 before, /device:TPU:97 now
where the time goes in v6:
time: 47.7 us; the launch traced here: 47.6 us
  Pallas kernels  46.8 us (98%)
  local copies, waits for them, and re-layouts  0.8 us (2%)
    pallas_call x1, Pallas kernels, shards(): pl.pallas_call(functools.partial(kernel, inner), in_specs=[SMEM, HBM, HBM...  46.8 us

profile of v6, /device:TPU:97, one launch (start us, length us, event | category | flops | bytes accessed | tf_op | source)
XLA Modules:
  0.0 47.6 jit_solution(12883765461396596203)
XLA Ops:
  0.0 46.8 %back_transform.1 = f32[64,2048]{1,0:T(8,128)S(1)} custom-call(s32[2]{0:T(128)} %offset_ref.1, f32[64,2048]{1,0:T(8,128)} %panel_ref.1, f32[256,256]{1,0:T(8,128)} %cauchy_ref.1, f32[2,16,256,128]{3,2,1,0:T(8,128)} %v_ref.1), custom_call_target="tpu_custom_call" | custom-call | tf_op jit(solution)/shard_map/back_transform/pallas_call | solution.py:711
  46.8 0.8 %copy.6 = f32[64,2048]{1,0:T(8,128)} copy(f32[64,2048]{1,0:T(8,128)S(1)} %back_transform.1) | data formatting | bytes 1048576
